TPU v7x, 32 devices: a whole 2x2x4 slice. The times are simulated.
32 devices in a mesh: layer: 4 (over z), row: 2 (over x), col: 4 (over y, core).
Axes of the slice: x: 2, y: 2, z: 4, core: 2. Of those that a mesh axis runs over, the one named last changes fastest.
Arguments:
- cost_vector: float32 [8, 1024, 512], P('layer', 'row', 'col'), may hold values from -12 to 12
- metal_density: float32 [8, 1024, 512], P('layer', 'row', 'col'), may hold values from 0 to 0.5
- cap_class: int32 [8, 1024, 512], P('layer', 'row', 'col'), may hold values from 0 to 7
- blocked_mask: int32 [8, 1024, 512], P('layer', 'row', 'col'), may hold values 0 or 1
- fill_start: float32 [8, 1024, 512], P('layer', 'row', 'col'), may hold values from 0 to 1
- window_dual: float32 [8, 1024, 512], P('layer', 'row', 'col'), may hold values from -4 to 4
- layer_dual: float32 [8, 1024, 512], P('layer', 'row', 'col'), may hold values from -4 to 4
Outputs:
- fill_level: float32 [8, 1024, 512], P('layer', 'row', 'col')
- window_price: float32 [8, 1024, 512], P('layer', 'row', 'col')
- layer_price: float32 [8, 1024, 512], P('layer', 'row', 'col')
- primal_weight: float32 [], replicated
All inputs are finite; a program needn't handle non-finite values. No bound on the sum of `blocked_mask` on one device may be relied on, other than what follows from the above.
Results may differ from a plain program's by a relative error of at most 0.00011.
Values sent between devices are 32-bit elements; how exact they have to be, the bound alone decides.
A program may use at most 64 MiB of HBM per device.

v0:
```python
import jax
import jax.numpy as jnp
from jax import lax
from jax.sharding import PartitionSpec as P

WIN = 50
CAP_LEVELS = 8
ITERS = 3
step_eta = 0.4
low_density = 0.35
high_density = 0.65
layer_gap = 0.15
tiny_term = 1e-06


def extended(cells, sides, width):
    for axis, dim in sides:
        count = lax.axis_size(axis)
        ends = count - 1
        head = lax.slice_in_dim(cells, 0, width, axis=dim)
        tail = lax.slice_in_dim(cells, cells.shape[dim] - width, cells.shape[dim], axis=dim)
        cells = jnp.concatenate(
            [
                lax.ppermute(tail, axis, [(i, (i + 1) % count) for i in range(ends)]),
                cells,
                lax.ppermute(head, axis, [((i + 1) % count, i) for i in range(ends)]),
            ],
            axis=dim,
        )
    return cells


def from_behind(block, axis, distance):
    devices = range(lax.axis_size(axis))
    route = [(i - distance, i) for i in devices if i - distance in devices]
    return lax.ppermute(block, axis, route)


def band_matrix(extent_out, extent_in, offset):
    index_out = lax.broadcasted_iota(jnp.int32, (extent_out, extent_in), 0)
    index_in = lax.broadcasted_iota(jnp.int32, (extent_out, extent_in), 1)
    spread = index_in - index_out
    return ((spread >= offset) & (spread < offset + WIN)).astype(jnp.float32)


def rows_pass(row_band, padded):
    return jnp.einsum("ip,lpq->liq", row_band, padded, precision=lax.Precision.HIGHEST)


def cols_pass(partial_sum, col_band):
    return jnp.einsum("liq,qj->lij", partial_sum, col_band, precision=lax.Precision.HIGHEST)


def fill_window(level, row_band, col_band, halfway):
    tall = extended(level, (("row", 1),), halfway)
    partial_sum = rows_pass(row_band, tall)
    wide = extended(partial_sum, (("col", 2),), halfway)
    result = cols_pass(wide, col_band)
    return result


def dual_window(density_dual, row_band, col_band, halfway):
    tall = extended(density_dual, (("row", 1),), halfway)
    partial_sum = rows_pass(row_band, tall)
    wide = extended(partial_sum, (("col", 2),), halfway)
    result = cols_pass(wide, col_band)
    return result


def local(cost_vector, metal_density, cap_class, blocked_mask, fill_start, window_dual, layer_dual):
    layers_here, row_count, col_count = fill_start.shape
    halfway = WIN // 2
    inverse_area = 1.0 / (WIN * WIN)
    row_forward = band_matrix(row_count, row_count + 2 * halfway, 0)
    row_backward = band_matrix(row_count, row_count + 2 * halfway, 1)
    col_forward = band_matrix(col_count, col_count + 2 * halfway, 0).T
    col_backward = band_matrix(col_count, col_count + 2 * halfway, 1).T
    layer_ids = lax.axis_index("layer") * layers_here + lax.iota(jnp.int32, layers_here)
    keep_mask = (layer_ids < lax.axis_size("layer") * layers_here - 1).astype(jnp.float32)[
        :, None, None
    ]
    capacity = jnp.where(blocked_mask == 1, 0.0, (cap_class + 1).astype(jnp.float32) / CAP_LEVELS)
    has_floor = blocked_mask == 0
    filling = fill_start
    density_dual = window_dual
    stacked_dual = layer_dual * keep_mask
    weight = jnp.float32(1.0)
    for iteration in range(ITERS):
        primal_step = step_eta / weight
        dual_step = step_eta * weight
        below = from_behind(stacked_dual[layers_here - 1 :], "layer", 1)
        earlier = jnp.concatenate([below, stacked_dual[: layers_here - 1]], axis=0)
        transposed = dual_window(density_dual, row_backward, col_backward, halfway)
        gradient = cost_vector + transposed * inverse_area + (stacked_dual - earlier)
        fill_new = jnp.clip(filling - primal_step * gradient, 0.0, capacity)
        moved = fill_new - filling
        primal_sum = jnp.sum(moved * moved)
        level = fill_new + moved + metal_density
        above = from_behind(level[0:1], "layer", -1)
        later = jnp.concatenate([level[1:], above], axis=0)
        forward = fill_window(level, row_forward, col_forward, halfway)
        window_term = density_dual / dual_step + forward * inverse_area
        capped = jnp.minimum(window_term, high_density)
        clipped = jnp.where(has_floor, jnp.maximum(capped, low_density), capped)
        density_new = dual_step * (window_term - clipped)
        layer_term = stacked_dual / dual_step + keep_mask * (level - later)
        stacked_new = (
            dual_step * (layer_term - jnp.clip(layer_term, -layer_gap, layer_gap)) * keep_mask
        )
        density_move = density_new - density_dual
        stacked_move = stacked_new - stacked_dual
        dual_sum = jnp.sum(density_move * density_move) + jnp.sum(stacked_move * stacked_move)
        primal_sum, dual_sum = lax.psum((primal_sum, dual_sum), ("layer", "row", "col"))
        weight = jnp.sqrt(weight) * jnp.sqrt(
            jnp.sqrt((dual_sum + tiny_term) / (primal_sum + tiny_term))
        )
        filling = fill_new
        density_dual = density_new
        stacked_dual = stacked_new
    return (filling, density_dual, stacked_dual, weight)


def solution(mesh):
    in_specs = (
        P("layer", "row", "col"),
        P("layer", "row", "col"),
        P("layer", "row", "col"),
        P("layer", "row", "col"),
        P("layer", "row", "col"),
        P("layer", "row", "col"),
        P("layer", "row", "col"),
    )
    out_specs = (P("layer", "row", "col"), P("layer", "row", "col"), P("layer", "row", "col"), P())
    return jax.shard_map(local, mesh=mesh, in_specs=in_specs, out_specs=out_specs, check_vma=False)
```

profile of v0, /device:TPU:0, one launch (start us, length us, event | category | flops | bytes accessed | tf_op | source)
XLA Modules:
  0.0 268.0 jit_solution(12571616555059935040)
XLA Ops:
  1.4 4.9 %collective-permute-start = (f32[2,25,128]{2,1,0:T(8,128)S(1)}, f32[2,25,128]{2,1,0:T(8,128)S(1)}, u32[]{:S(2)}, u32[]{:S(2)}) collective-permute-start(f32[2,25,128]{2,1,0:T(8,128)S(1)} %get-tuple-element.56), channel_id=1, source_target_pairs={{0,4},{1,5},{2,6},{3,7},{8,12},{9,13},{10,14},{11,15},{16,20},{17,... | collective-permute-start | bytes 76808 | tf_op jit(solution)/shard_map/ppermute | solution.py:24
  8.8 3.6 %collective-permute-start.4 = (f32[1,512,128]{2,1,0:T(8,128)S(1)}, f32[1,512,128]{2,1,0:T(8,128)S(1)}, u32[]{:S(2)}, u32[]{:S(2)}) collective-permute-start(f32[1,512,128]{2,1,0:T(8,128)S(1)} %get-tuple-element.52), channel_id=1, source_target_pairs={{0,8},{8,16},{16,24},{1,9},{9,17},{17,25},{2,10},{10,18},{18,26},{... | collective-permute-start | bytes 786440 | tf_op jit(solution)/shard_map/ppermute | solution.py:36
  16.2 3.7 %collective-permute-done.3 = f32[2,512,25]{1,2,0:T(8,128)S(1)} collective-permute-done((f32[2,512,25]{1,2,0:T(8,128)S(1)}, f32[2,512,25]{1,2,0:T(8,128)S(1)}, u32[]{:S(2)}, u32[]{:S(2)}) %collective-permute-start.3) | collective-permute-done | bytes 102432 | tf_op jit(solution)/shard_map/ppermute | solution.py:26
  20.0 2.5 multiply_reduce_fusion.6
  22.5 4.5 %collective-permute-start.5 = (f32[2,25,128]{2,1,0:T(8,128)S(1)}, f32[2,25,128]{2,1,0:T(8,128)S(1)}, u32[]{:S(2)}, u32[]{:S(2)}) collective-permute-start(f32[2,25,128]{2,1,0:T(8,128)S(1)} %get-tuple-element.50), channel_id=1, source_target_pairs={{0,4},{1,5},{2,6},{3,7},{8,12},{9,13},{10,14},{11,15},{16,20},{17,... | collective-permute-start | bytes 76808 | tf_op jit(solution)/shard_map/ppermute | solution.py:24
  28.6 4.2 %collective-permute-done.6 = f32[2,25,128]{2,1,0:T(8,128)S(1)} collective-permute-done((f32[2,25,128]{2,1,0:T(8,128)S(1)}, f32[2,25,128]{2,1,0:T(8,128)S(1)}, u32[]{:S(2)}, u32[]{:S(2)}) %collective-permute-start.6) | collective-permute-done | bytes 25632 | tf_op jit(solution)/shard_map/ppermute | solution.py:26
  33.8 4.0 %collective-permute-start.7 = (f32[2,512,25]{1,2,0:T(8,128)S(1)}, f32[2,512,25]{1,2,0:T(8,128)S(1)}, u32[]{:S(2)}, u32[]{:S(2)}) collective-permute-start(f32[2,512,25]{1,2,0:T(8,128)S(1)} %get-tuple-element.48), channel_id=1, source_target_pairs={{0,1},{1,2},{2,3},{4,5},{5,6},{6,7},{8,9},{9,10},{10,11},{12,13},{... | collective-permute-start | bytes 307208 | tf_op jit(solution)/shard_map/ppermute | solution.py:24
  41.9 1.7 multiply_reduce_fusion.8
  43.6 1.6 collective-permute-start.10
  46.8 4.2 %collective-permute-done.11 = f32[2,25,128]{2,1,0:T(8,128)S(1)} collective-permute-done((f32[2,25,128]{2,1,0:T(8,128)S(1)}, f32[2,25,128]{2,1,0:T(8,128)S(1)}, u32[]{:S(2)}, u32[]{:S(2)}) %collective-permute-start.11) | collective-permute-done | bytes 25632 | tf_op jit(solution)/shard_map/ppermute | solution.py:26
  52.9 3.5 %collective-permute-start.14 = (f32[1,512,128]{2,1,0:T(8,128)S(1)}, f32[1,512,128]{2,1,0:T(8,128)S(1)}, u32[]{:S(2)}, u32[]{:S(2)}) collective-permute-start(f32[1,512,128]{2,1,0:T(8,128)S(1)} %get-tuple-element.40), channel_id=1, source_target_pairs={{0,8},{8,16},{16,24},{1,9},{9,17},{17,25},{2,10},{10,18},{18,26},{... | collective-permute-start | bytes 786440 | tf_op jit(solution)/shard_map/ppermute | solution.py:36
  57.2 4.7 %collective-permute-start.12 = (f32[2,512,25]{1,2,0:T(8,128)}, f32[2,512,25]{1,2,0:T(8,128)}, u32[]{:S(2)}, u32[]{:S(2)}) collective-permute-start(f32[2,512,25]{1,2,0:T(8,128)} %get-tuple-element.44), channel_id=1, source_target_pairs={{0,1},{1,2},{2,3},{4,5},{5,6},{6,7},{8,9},{9,10},{10,11},{12,13},{... | collective-permute-start | bytes 307208 | tf_op jit(solution)/shard_map/ppermute | solution.py:24
  64.4 40.6 %all-reduce.2 = (f32[]{:T(128)}, f32[]{:T(128)}) all-reduce(f32[]{:T(128)S(6)} %add.115, f32[]{:T(128)} %get-tuple-element.20), channel_id=1, replica_groups=mesh['layer'=4,'row'=2,'col'=4] {'layer','row','col'}, use_global_device_ids=true, to_apply=%region_2.3 | all-reduce | flops 2 | bytes 16 | tf_op jit(solution)/shard_map/psum | solution.py:113
  107.2 3.9 %multiply_reduce_fusion.3 = (f32[]{:T(128)}, f32[2,512,128]{2,1,0:T(8,128)S(1)}, f32[2,512,128]{2,1,0:T(8,128)}) fusion(f32[2,512,128]{2,1,0:T(8,128)} %get-tuple-element.58, f32[2,512,128]{2,1,0:T(8,128)S(1)} %copy-done.1, f32[2,512,128]{2,1,0:T(8,128)S(1)} %get-tuple-element.15, f32[1,512,128]{2,1,0:T(8,128)S(1)} %get-tuple-element.41, ...), kind=kOutput, calls=%fused_computation.139 | convolution fusion | flops 282915840 | bytes 5447688 | tf_op jit(solution)/shard_map/liq,qj->lij/dot_general | solution.py:51
  111.1 4.2 %collective-permute-start.15 = (f32[2,25,128]{2,1,0:T(8,128)S(1)}, f32[2,25,128]{2,1,0:T(8,128)S(1)}, u32[]{:S(2)}, u32[]{:S(2)}) collective-permute-start(f32[2,25,128]{2,1,0:T(8,128)S(1)} %get-tuple-element.38), channel_id=1, source_target_pairs={{0,4},{1,5},{2,6},{3,7},{8,12},{9,13},{10,14},{11,15},{16,20},{17,... | collective-permute-start | bytes 76808 | tf_op jit(solution)/shard_map/ppermute | solution.py:24
  116.8 4.2 %collective-permute-done.16 = f32[2,25,128]{2,1,0:T(8,128)S(1)} collective-permute-done((f32[2,25,128]{2,1,0:T(8,128)S(1)}, f32[2,25,128]{2,1,0:T(8,128)S(1)}, u32[]{:S(2)}, u32[]{:S(2)}) %collective-permute-start.16) | collective-permute-done | bytes 25632 | tf_op jit(solution)/shard_map/ppermute | solution.py:26
  126.1 2.9 %collective-permute-done.18 = f32[2,512,25]{1,2,0:T(8,128)S(1)} collective-permute-done((f32[2,512,25]{1,2,0:T(8,128)S(1)}, f32[2,512,25]{1,2,0:T(8,128)S(1)}, u32[]{:S(2)}, u32[]{:S(2)}) %collective-permute-start.18) | collective-permute-done | bytes 102432 | tf_op jit(solution)/shard_map/ppermute | solution.py:26
  129.0 1.7 multiply_reduce_fusion.5
  130.8 1.6 collective-permute-start.20
  132.4 1.5 collective-permute-start.21
  134.0 4.2 %collective-permute-done.21 = f32[2,25,128]{2,1,0:T(8,128)S(1)} collective-permute-done((f32[2,25,128]{2,1,0:T(8,128)S(1)}, f32[2,25,128]{2,1,0:T(8,128)S(1)}, u32[]{:S(2)}, u32[]{:S(2)}) %collective-permute-start.21) | collective-permute-done | bytes 25632 | tf_op jit(solution)/shard_map/ppermute | solution.py:26
  140.2 2.4 collective-permute-start.24
  143.3 4.7 %collective-permute-start.22 = (f32[2,512,25]{1,2,0:T(8,128)}, f32[2,512,25]{1,2,0:T(8,128)}, u32[]{:S(2)}, u32[]{:S(2)}) collective-permute-start(f32[2,512,25]{1,2,0:T(8,128)} %get-tuple-element.32), channel_id=1, source_target_pairs={{0,1},{1,2},{2,3},{4,5},{5,6},{6,7},{8,9},{9,10},{10,11},{12,13},{... | collective-permute-start | bytes 307208 | tf_op jit(solution)/shard_map/ppermute | solution.py:24
  150.6 40.6 %all-reduce.1 = (f32[]{:T(128)}, f32[]{:T(128)}) all-reduce(f32[]{:T(128)S(6)} %add.124, f32[]{:T(128)} %get-tuple-element.18), channel_id=1, replica_groups=mesh['layer'=4,'row'=2,'col'=4] {'layer','row','col'}, use_global_device_ids=true, to_apply=%region_7.8 | all-reduce | flops 2 | bytes 16 | tf_op jit(solution)/shard_map/psum | solution.py:113
  193.4 3.9 %multiply_reduce_fusion = (f32[]{:T(128)}, f32[2,512,128]{2,1,0:T(8,128)S(1)}, f32[2,512,128]{2,1,0:T(8,128)}) fusion(f32[2,512,128]{2,1,0:T(8,128)} %get-tuple-element.61, f32[2,512,128]{2,1,0:T(8,128)S(1)} %copy-done.1, f32[2,512,128]{2,1,0:T(8,128)S(1)} %get-tuple-element.13, f32[1,512,128]{2,1,0:T(8,128)S(1)} %get-tuple-element.29, ...), kind=kOutput, calls=%fused_computation.134 | convolution fusion | flops 282915840 | bytes 5447688 | tf_op jit(solution)/shard_map/liq,qj->lij/dot_general | solution.py:51
  197.3 4.2 %collective-permute-start.25 = (f32[2,25,128]{2,1,0:T(8,128)S(1)}, f32[2,25,128]{2,1,0:T(8,128)S(1)}, u32[]{:S(2)}, u32[]{:S(2)}) collective-permute-start(f32[2,25,128]{2,1,0:T(8,128)S(1)} %get-tuple-element.26), channel_id=1, source_target_pairs={{0,4},{1,5},{2,6},{3,7},{8,12},{9,13},{10,14},{11,15},{16,20},{17,... | collective-permute-start | bytes 76808 | tf_op jit(solution)/shard_map/ppermute | solution.py:24
  203.1 4.2 %collective-permute-done.26 = f32[2,25,128]{2,1,0:T(8,128)S(1)} collective-permute-done((f32[2,25,128]{2,1,0:T(8,128)S(1)}, f32[2,25,128]{2,1,0:T(8,128)S(1)}, u32[]{:S(2)}, u32[]{:S(2)}) %collective-permute-start.26) | collective-permute-done | bytes 25632 | tf_op jit(solution)/shard_map/ppermute | solution.py:26
  212.4 2.9 %collective-permute-done.28 = f32[2,512,25]{1,2,0:T(8,128)S(1)} collective-permute-done((f32[2,512,25]{1,2,0:T(8,128)S(1)}, f32[2,512,25]{1,2,0:T(8,128)S(1)}, u32[]{:S(2)}, u32[]{:S(2)}) %collective-permute-start.28) | collective-permute-done | bytes 102432 | tf_op jit(solution)/shard_map/ppermute | solution.py:26
  215.3 2.5 multiply_reduce_fusion.2
  217.8 1.8 collective-permute-done.29
  219.6 1.7 multiply_reduce_fusion.1
  222.5 43.0 %all-reduce = (f32[]{:T(128)}, f32[]{:T(128)}) all-reduce(f32[]{:T(128)S(6)} %add.133, f32[]{:T(128)} %get-tuple-element.16), channel_id=1, replica_groups=mesh['layer'=4,'row'=2,'col'=4] {'layer','row','col'}, use_global_device_ids=true, to_apply=%region_12.13 | all-reduce | flops 2 | bytes 16 | tf_op jit(solution)/shard_map/psum | solution.py:113
  (100 shorter events, 37.5 us)
Async XLA Ops:
  1.4 11.0 %collective-permute-start = (f32[2,25,128]{2,1,0:T(8,128)S(1)}, f32[2,25,128]{2,1,0:T(8,128)S(1)}, u32[]{:S(2)}, u32[]{:S(2)}) collective-permute-start(f32[2,25,128]{2,1,0:T(8,128)S(1)} %get-tuple-element.56), channel_id=1, source_target_pairs={{0,4},{1,5},{2,6},{3,7},{8,12},{9,13},{10,14},{11,15},{16,20},{17,... | collective-permute-start | bytes 76808 | tf_op jit(solution)/shard_map/ppermute | solution.py:24
  6.3 6.2 %collective-permute-start.1 = (f32[2,25,128]{2,1,0:T(8,128)S(1)}, f32[2,25,128]{2,1,0:T(8,128)S(1)}, u32[]{:S(2)}, u32[]{:S(2)}) collective-permute-start(f32[2,25,128]{2,1,0:T(8,128)S(1)} %get-tuple-element.57), channel_id=1, source_target_pairs={{4,0},{5,1},{6,2},{7,3},{12,8},{13,9},{14,10},{15,11},{20,16},{21,... | collective-permute-start | bytes 76808 | tf_op jit(solution)/shard_map/ppermute | solution.py:26
  8.8 11.1 %collective-permute-start.4 = (f32[1,512,128]{2,1,0:T(8,128)S(1)}, f32[1,512,128]{2,1,0:T(8,128)S(1)}, u32[]{:S(2)}, u32[]{:S(2)}) collective-permute-start(f32[1,512,128]{2,1,0:T(8,128)S(1)} %get-tuple-element.52), channel_id=1, source_target_pairs={{0,8},{8,16},{16,24},{1,9},{9,17},{17,25},{2,10},{10,18},{18,26},{... | collective-permute-start | bytes 786440 | tf_op jit(solution)/shard_map/ppermute | solution.py:36
  13.5 2.7 %collective-permute-start.2 = (f32[2,512,25]{1,2,0:T(8,128)S(1)}, f32[2,512,25]{1,2,0:T(8,128)S(1)}, u32[]{:S(2)}, u32[]{:S(2)}) collective-permute-start(f32[2,512,25]{1,2,0:T(8,128)S(1)} %get-tuple-element.54), channel_id=1, source_target_pairs={{0,1},{1,2},{2,3},{4,5},{5,6},{6,7},{8,9},{9,10},{10,11},{12,13},{... | collective-permute-start | bytes 307208 | tf_op jit(solution)/shard_map/ppermute | solution.py:24
  14.9 5.0 %collective-permute-start.3 = (f32[2,512,25]{1,2,0:T(8,128)S(1)}, f32[2,512,25]{1,2,0:T(8,128)S(1)}, u32[]{:S(2)}, u32[]{:S(2)}) collective-permute-start(f32[2,512,25]{1,2,0:T(8,128)S(1)} %get-tuple-element.55), channel_id=1, source_target_pairs={{1,0},{2,1},{3,2},{5,4},{6,5},{7,6},{9,8},{10,9},{11,10},{13,12},{... | collective-permute-start | bytes 307208 | tf_op jit(solution)/shard_map/ppermute | solution.py:26
  22.5 6.1 %collective-permute-start.5 = (f32[2,25,128]{2,1,0:T(8,128)S(1)}, f32[2,25,128]{2,1,0:T(8,128)S(1)}, u32[]{:S(2)}, u32[]{:S(2)}) collective-permute-start(f32[2,25,128]{2,1,0:T(8,128)S(1)} %get-tuple-element.50), channel_id=1, source_target_pairs={{0,4},{1,5},{2,6},{3,7},{8,12},{9,13},{10,14},{11,15},{16,20},{17,... | collective-permute-start | bytes 76808 | tf_op jit(solution)/shard_map/ppermute | solution.py:24
  27.0 5.8 %collective-permute-start.6 = (f32[2,25,128]{2,1,0:T(8,128)S(1)}, f32[2,25,128]{2,1,0:T(8,128)S(1)}, u32[]{:S(2)}, u32[]{:S(2)}) collective-permute-start(f32[2,25,128]{2,1,0:T(8,128)S(1)} %get-tuple-element.51), channel_id=1, source_target_pairs={{4,0},{5,1},{6,2},{7,3},{12,8},{13,9},{14,10},{15,11},{20,16},{21,... | collective-permute-start | bytes 76808 | tf_op jit(solution)/shard_map/ppermute | solution.py:26
  33.8 6.7 %collective-permute-start.7 = (f32[2,512,25]{1,2,0:T(8,128)S(1)}, f32[2,512,25]{1,2,0:T(8,128)S(1)}, u32[]{:S(2)}, u32[]{:S(2)}) collective-permute-start(f32[2,512,25]{1,2,0:T(8,128)S(1)} %get-tuple-element.48), channel_id=1, source_target_pairs={{0,1},{1,2},{2,3},{4,5},{5,6},{6,7},{8,9},{9,10},{10,11},{12,13},{... | collective-permute-start | bytes 307208 | tf_op jit(solution)/shard_map/ppermute | solution.py:24
  37.8 4.0 %collective-permute-start.8 = (f32[2,512,25]{1,2,0:T(8,128)S(1)}, f32[2,512,25]{1,2,0:T(8,128)S(1)}, u32[]{:S(2)}, u32[]{:S(2)}) collective-permute-start(f32[2,512,25]{1,2,0:T(8,128)S(1)} %get-tuple-element.49), channel_id=1, source_target_pairs={{1,0},{2,1},{3,2},{5,4},{6,5},{7,6},{9,8},{10,9},{11,10},{13,12},{... | collective-permute-start | bytes 307208 | tf_op jit(solution)/shard_map/ppermute | solution.py:26
  39.2 12.8 %collective-permute-start.9 = (f32[1,512,128]{2,1,0:T(8,128)S(1)}, f32[1,512,128]{2,1,0:T(8,128)S(1)}, u32[]{:S(2)}, u32[]{:S(2)}) collective-permute-start(f32[1,512,128]{2,1,0:T(8,128)S(1)} %get-tuple-element.43), channel_id=1, source_target_pairs={{8,0},{16,8},{24,16},{9,1},{17,9},{25,17},{10,2},{18,10},{26,18},{... | collective-permute-start | bytes 786440 | tf_op jit(solution)/shard_map/ppermute | solution.py:36
  43.6 8.4 %copy-start.14 = (f32[2,512,128]{2,1,0:T(8,128)}, f32[2,512,128]{2,1,0:T(8,128)S(1)}, u32[]{:S(2)}) copy-start(f32[2,512,128]{2,1,0:T(8,128)S(1)} %get-tuple-element.60) | copy-start | bytes 1572868
  43.6 3.2 %collective-permute-start.10 = (f32[2,25,128]{2,1,0:T(8,128)S(1)}, f32[2,25,128]{2,1,0:T(8,128)S(1)}, u32[]{:S(2)}, u32[]{:S(2)}) collective-permute-start(f32[2,25,128]{2,1,0:T(8,128)S(1)} %get-tuple-element.46), channel_id=1, source_target_pairs={{0,4},{1,5},{2,6},{3,7},{8,12},{9,13},{10,14},{11,15},{16,20},{17,... | collective-permute-start | bytes 76808 | tf_op jit(solution)/shard_map/ppermute | solution.py:24
  45.2 5.8 %collective-permute-start.11 = (f32[2,25,128]{2,1,0:T(8,128)S(1)}, f32[2,25,128]{2,1,0:T(8,128)S(1)}, u32[]{:S(2)}, u32[]{:S(2)}) collective-permute-start(f32[2,25,128]{2,1,0:T(8,128)S(1)} %get-tuple-element.47), channel_id=1, source_target_pairs={{4,0},{5,1},{6,2},{7,3},{12,8},{13,9},{14,10},{15,11},{20,16},{21,... | collective-permute-start | bytes 76808 | tf_op jit(solution)/shard_map/ppermute | solution.py:26
  52.9 53.5 %collective-permute-start.14 = (f32[1,512,128]{2,1,0:T(8,128)S(1)}, f32[1,512,128]{2,1,0:T(8,128)S(1)}, u32[]{:S(2)}, u32[]{:S(2)}) collective-permute-start(f32[1,512,128]{2,1,0:T(8,128)S(1)} %get-tuple-element.40), channel_id=1, source_target_pairs={{0,8},{8,16},{16,24},{1,9},{9,17},{17,25},{2,10},{10,18},{18,26},{... | collective-permute-start | bytes 786440 | tf_op jit(solution)/shard_map/ppermute | solution.py:36
  57.2 49.2 %collective-permute-start.12 = (f32[2,512,25]{1,2,0:T(8,128)}, f32[2,512,25]{1,2,0:T(8,128)}, u32[]{:S(2)}, u32[]{:S(2)}) collective-permute-start(f32[2,512,25]{1,2,0:T(8,128)} %get-tuple-element.44), channel_id=1, source_target_pairs={{0,1},{1,2},{2,3},{4,5},{5,6},{6,7},{8,9},{9,10},{10,11},{12,13},{... | collective-permute-start | bytes 307208 | tf_op jit(solution)/shard_map/ppermute | solution.py:24
  61.9 44.6 %collective-permute-start.13 = (f32[2,512,25]{1,2,0:T(8,128)}, f32[2,512,25]{1,2,0:T(8,128)}, u32[]{:S(2)}, u32[]{:S(2)}) collective-permute-start(f32[2,512,25]{1,2,0:T(8,128)} %get-tuple-element.45), channel_id=1, source_target_pairs={{1,0},{2,1},{3,2},{5,4},{6,5},{7,6},{9,8},{10,9},{11,10},{13,12},{... | collective-permute-start | bytes 307208 | tf_op jit(solution)/shard_map/ppermute | solution.py:26
  111.1 5.8 %collective-permute-start.15 = (f32[2,25,128]{2,1,0:T(8,128)S(1)}, f32[2,25,128]{2,1,0:T(8,128)S(1)}, u32[]{:S(2)}, u32[]{:S(2)}) collective-permute-start(f32[2,25,128]{2,1,0:T(8,128)S(1)} %get-tuple-element.38), channel_id=1, source_target_pairs={{0,4},{1,5},{2,6},{3,7},{8,12},{9,13},{10,14},{11,15},{16,20},{17,... | collective-permute-start | bytes 76808 | tf_op jit(solution)/shard_map/ppermute | solution.py:24
  115.2 5.8 %collective-permute-start.16 = (f32[2,25,128]{2,1,0:T(8,128)S(1)}, f32[2,25,128]{2,1,0:T(8,128)S(1)}, u32[]{:S(2)}, u32[]{:S(2)}) collective-permute-start(f32[2,25,128]{2,1,0:T(8,128)S(1)} %get-tuple-element.39), channel_id=1, source_target_pairs={{4,0},{5,1},{6,2},{7,3},{12,8},{13,9},{14,10},{15,11},{20,16},{21,... | collective-permute-start | bytes 76808 | tf_op jit(solution)/shard_map/ppermute | solution.py:26
  122.0 4.1 %collective-permute-start.17 = (f32[2,512,25]{1,2,0:T(8,128)S(1)}, f32[2,512,25]{1,2,0:T(8,128)S(1)}, u32[]{:S(2)}, u32[]{:S(2)}) collective-permute-start(f32[2,512,25]{1,2,0:T(8,128)S(1)} %get-tuple-element.36), channel_id=1, source_target_pairs={{0,1},{1,2},{2,3},{4,5},{5,6},{6,7},{8,9},{9,10},{10,11},{12,13},{... | collective-permute-start | bytes 307208 | tf_op jit(solution)/shard_map/ppermute | solution.py:24
  123.3 5.7 %collective-permute-start.18 = (f32[2,512,25]{1,2,0:T(8,128)S(1)}, f32[2,512,25]{1,2,0:T(8,128)S(1)}, u32[]{:S(2)}, u32[]{:S(2)}) collective-permute-start(f32[2,512,25]{1,2,0:T(8,128)S(1)} %get-tuple-element.37), channel_id=1, source_target_pairs={{1,0},{2,1},{3,2},{5,4},{6,5},{7,6},{9,8},{10,9},{11,10},{13,12},{... | collective-permute-start | bytes 307208 | tf_op jit(solution)/shard_map/ppermute | solution.py:26
  124.8 14.4 %collective-permute-start.19 = (f32[1,512,128]{2,1,0:T(8,128)S(1)}, f32[1,512,128]{2,1,0:T(8,128)S(1)}, u32[]{:S(2)}, u32[]{:S(2)}) collective-permute-start(f32[1,512,128]{2,1,0:T(8,128)S(1)} %get-tuple-element.31), channel_id=1, source_target_pairs={{8,0},{16,8},{24,16},{9,1},{17,9},{25,17},{10,2},{18,10},{26,18},{... | collective-permute-start | bytes 786440 | tf_op jit(solution)/shard_map/ppermute | solution.py:36
  130.8 3.2 %collective-permute-start.20 = (f32[2,25,128]{2,1,0:T(8,128)S(1)}, f32[2,25,128]{2,1,0:T(8,128)S(1)}, u32[]{:S(2)}, u32[]{:S(2)}) collective-permute-start(f32[2,25,128]{2,1,0:T(8,128)S(1)} %get-tuple-element.34), channel_id=1, source_target_pairs={{0,4},{1,5},{2,6},{3,7},{8,12},{9,13},{10,14},{11,15},{16,20},{17,... | collective-permute-start | bytes 76808 | tf_op jit(solution)/shard_map/ppermute | solution.py:24
  132.4 5.8 %collective-permute-start.21 = (f32[2,25,128]{2,1,0:T(8,128)S(1)}, f32[2,25,128]{2,1,0:T(8,128)S(1)}, u32[]{:S(2)}, u32[]{:S(2)}) collective-permute-start(f32[2,25,128]{2,1,0:T(8,128)S(1)} %get-tuple-element.35), channel_id=1, source_target_pairs={{4,0},{5,1},{6,2},{7,3},{12,8},{13,9},{14,10},{15,11},{20,16},{21,... | collective-permute-start | bytes 76808 | tf_op jit(solution)/shard_map/ppermute | solution.py:26
  140.2 53.2 %copy-start.4 = (s32[2,512,128]{2,1,0:T(8,128)S(1)}, s32[2,512,128]{2,1,0:T(8,128)}, u32[]{:S(2)}) copy-start(s32[2,512,128]{2,1,0:T(8,128)} %param.9) | copy-start | bytes 1572868
  140.2 52.5 %collective-permute-start.24 = (f32[1,512,128]{2,1,0:T(8,128)S(1)}, f32[1,512,128]{2,1,0:T(8,128)S(1)}, u32[]{:S(2)}, u32[]{:S(2)}) collective-permute-start(f32[1,512,128]{2,1,0:T(8,128)S(1)} %get-tuple-element.28), channel_id=1, source_target_pairs={{0,8},{8,16},{16,24},{1,9},{9,17},{17,25},{2,10},{10,18},{18,26},{... | collective-permute-start | bytes 786440 | tf_op jit(solution)/shard_map/ppermute | solution.py:36
  143.3 49.4 %collective-permute-start.22 = (f32[2,512,25]{1,2,0:T(8,128)}, f32[2,512,25]{1,2,0:T(8,128)}, u32[]{:S(2)}, u32[]{:S(2)}) collective-permute-start(f32[2,512,25]{1,2,0:T(8,128)} %get-tuple-element.32), channel_id=1, source_target_pairs={{0,1},{1,2},{2,3},{4,5},{5,6},{6,7},{8,9},{9,10},{10,11},{12,13},{... | collective-permute-start | bytes 307208 | tf_op jit(solution)/shard_map/ppermute | solution.py:24
  148.0 44.7 %collective-permute-start.23 = (f32[2,512,25]{1,2,0:T(8,128)}, f32[2,512,25]{1,2,0:T(8,128)}, u32[]{:S(2)}, u32[]{:S(2)}) collective-permute-start(f32[2,512,25]{1,2,0:T(8,128)} %get-tuple-element.33), channel_id=1, source_target_pairs={{1,0},{2,1},{3,2},{5,4},{6,5},{7,6},{9,8},{10,9},{11,10},{13,12},{... | collective-permute-start | bytes 307208 | tf_op jit(solution)/shard_map/ppermute | solution.py:26
  197.3 5.8 %collective-permute-start.25 = (f32[2,25,128]{2,1,0:T(8,128)S(1)}, f32[2,25,128]{2,1,0:T(8,128)S(1)}, u32[]{:S(2)}, u32[]{:S(2)}) collective-permute-start(f32[2,25,128]{2,1,0:T(8,128)S(1)} %get-tuple-element.26), channel_id=1, source_target_pairs={{0,4},{1,5},{2,6},{3,7},{8,12},{9,13},{10,14},{11,15},{16,20},{17,... | collective-permute-start | bytes 76808 | tf_op jit(solution)/shard_map/ppermute | solution.py:24
  201.5 5.8 %collective-permute-start.26 = (f32[2,25,128]{2,1,0:T(8,128)S(1)}, f32[2,25,128]{2,1,0:T(8,128)S(1)}, u32[]{:S(2)}, u32[]{:S(2)}) collective-permute-start(f32[2,25,128]{2,1,0:T(8,128)S(1)} %get-tuple-element.27), channel_id=1, source_target_pairs={{4,0},{5,1},{6,2},{7,3},{12,8},{13,9},{14,10},{15,11},{20,16},{21,... | collective-permute-start | bytes 76808 | tf_op jit(solution)/shard_map/ppermute | solution.py:26
  208.2 4.1 %collective-permute-start.27 = (f32[2,512,25]{1,2,0:T(8,128)S(1)}, f32[2,512,25]{1,2,0:T(8,128)S(1)}, u32[]{:S(2)}, u32[]{:S(2)}) collective-permute-start(f32[2,512,25]{1,2,0:T(8,128)S(1)} %get-tuple-element.24), channel_id=1, source_target_pairs={{0,1},{1,2},{2,3},{4,5},{5,6},{6,7},{8,9},{9,10},{10,11},{12,13},{... | collective-permute-start | bytes 307208 | tf_op jit(solution)/shard_map/ppermute | solution.py:24
  209.5 5.7 %collective-permute-start.28 = (f32[2,512,25]{1,2,0:T(8,128)S(1)}, f32[2,512,25]{1,2,0:T(8,128)S(1)}, u32[]{:S(2)}, u32[]{:S(2)}) collective-permute-start(f32[2,512,25]{1,2,0:T(8,128)S(1)} %get-tuple-element.25), channel_id=1, source_target_pairs={{1,0},{2,1},{3,2},{5,4},{6,5},{7,6},{9,8},{10,9},{11,10},{13,12},{... | collective-permute-start | bytes 307208 | tf_op jit(solution)/shard_map/ppermute | solution.py:26
  211.0 8.6 %collective-permute-start.29 = (f32[1,512,128]{2,1,0:T(8,128)S(1)}, f32[1,512,128]{2,1,0:T(8,128)S(1)}, u32[]{:S(2)}, u32[]{:S(2)}) collective-permute-start(f32[1,512,128]{2,1,0:T(8,128)S(1)} %get-tuple-element.23), channel_id=1, source_target_pairs={{8,0},{16,8},{24,16},{9,1},{17,9},{25,17},{10,2},{18,10},{26,18},{... | collective-permute-start | bytes 786440 | tf_op jit(solution)/shard_map/ppermute | solution.py:36
  (14 other events, 74.5 us)
where the time goes:
time: 269 us; the launch traced here: 268 us
  blocking collectives  124 us (46%)
  starting transfers between devices  67.7 us (25%)
  waiting for transfers between devices  35 us (13%)
  matrix products  21.7 us (8%)
  between operations  10.6 us (4%)
  other arithmetic  4.76 us (2%)
  local copies, waits for them, and re-layouts  4.08 us (2%)
    psum x3, blocking collectives, local(): lax.psum((primal_sum, dual_sum), ('layer', 'row', 'col'))  124 us
    ppermute x12, starting transfers between devices, extended(): lax.ppermute(tail, axis, [(i, (i + 1) % count) for i in range(ends)])  38.4 us
    ppermute x12, waiting for transfers between devices, extended(): lax.ppermute(head, axis, [((i + 1) % count, i) for i in range(ends)])  32.1 us
    dot_general x6, matrix products, cols_pass(): jnp.einsum('liq,qj->lij', partial_sum, col_band, precision=lax.Precision....  16.3 us
    ppermute x12, starting transfers between devices, extended(): lax.ppermute(head, axis, [((i + 1) % count, i) for i in range(ends)])  15.9 us
    ppermute x6, starting transfers between devices, from_behind(): return lax.ppermute(block, axis, route)  13.4 us
    dot_general x6, matrix products, rows_pass(): jnp.einsum('ip,lpq->liq', row_band, padded, precision=lax.Precision.HIGHEST)  5.39 us
  transfers between devices with their start and end apart: 30, of which 15 were waited for; matrix products, arithmetic and copies ran while one was open for 4% of the time, Pallas kernels for 0%

commit v1 on v0

--- a/solution.py
+++ b/solution.py
@@ -2,6 +2,7 @@
 import jax.numpy as jnp
 from jax import lax
 from jax.sharding import PartitionSpec as P
+from jax.lax import psum
 
 WIN = 50
 CAP_LEVELS = 8
@@ -11,6 +12,12 @@
 high_density = 0.65
 layer_gap = 0.15
 tiny_term = 1e-06
+
+
+def mark_series_all(q_in):
+    for jj in ("layer", ("row", "col")):
+        q_in = psum(q_in, jj)
+    return q_in
 
 
 def extended(cells, sides, width):
@@ -110,7 +117,7 @@
         density_move = density_new - density_dual
         stacked_move = stacked_new - stacked_dual
         dual_sum = jnp.sum(density_move * density_move) + jnp.sum(stacked_move * stacked_move)
-        primal_sum, dual_sum = lax.psum((primal_sum, dual_sum), ("layer", "row", "col"))
+        primal_sum, dual_sum = mark_series_all((primal_sum, dual_sum))
         weight = jnp.sqrt(weight) * jnp.sqrt(
             jnp.sqrt((dual_sum + tiny_term) / (primal_sum + tiny_term))
         )

time: 269 us -> 211 us (0.78)
  blocking collectives: 124 us -> 69.2 us
    psum x3 -> x6, blocking collectives: 124 us -> 69.2 us  [mark_series_all(): q_in = psum(q_in, jj)]
    ppermute x6, waiting for transfers between devices: 1.77 us -> 6.5 us  [from_behind(): return lax.ppermute(block, axis, route)]
    ppermute x12, waiting for transfers between devices: 32.1 us -> 27.3 us  [extended(): lax.ppermute(head, axis, [((i + 1) % count, i) for i in range(ends)])]
    ppermute x12, starting transfers between devices: 38.4 us -> 34.4 us  [extended(): lax.ppermute(tail, axis, [(i, (i + 1) % count) for i in range(ends)])]
  transfers between devices with their start and end apart: 30 -> 30, of which waited for: 15 -> 15; matrix products, arithmetic and copies ran while one was open for 4% -> 5% of each run, Pallas kernels for 0% -> 0%
where the time goes in v1:
time: 211 us; the launch traced here: 210 us
  blocking collectives  69.2 us (33%)
  starting transfers between devices  65.4 us (31%)
  waiting for transfers between devices  35 us (17%)
  matrix products  21.7 us (10%)
  between operations  10.2 us (5%)
  other arithmetic  4.7 us (2%)
  local copies, waits for them, and re-layouts  4.03 us (2%)
    psum x6, blocking collectives, mark_series_all(): q_in = psum(q_in, jj)  69.2 us
    ppermute x12, starting transfers between devices, extended(): lax.ppermute(tail, axis, [(i, (i + 1) % count) for i in range(ends)])  34.4 us
    ppermute x12, waiting for transfers between devices, extended(): lax.ppermute(head, axis, [((i + 1) % count, i) for i in range(ends)])  27.3 us
    dot_general x6, matrix products, cols_pass(): jnp.einsum('liq,qj->lij', partial_sum, col_band, precision=lax.Precision....  16.3 us
    ppermute x12, starting transfers between devices, extended(): lax.ppermute(head, axis, [((i + 1) % count, i) for i in range(ends)])  15.9 us
    ppermute x6, starting transfers between devices, from_behind(): return lax.ppermute(block, axis, route)  15.1 us
    ppermute x6, waiting for transfers between devices, from_behind(): return lax.ppermute(block, axis, route)  6.5 us
    dot_general x6, matrix products, rows_pass(): jnp.einsum('ip,lpq->liq', row_band, padded, precision=lax.Precision.HIGHEST)  5.39 us
  transfers between devices with their start and end apart: 30, of which 15 were waited for; matrix products, arithmetic and copies ran while one was open for 5% of the time, Pallas kernels for 0%

profile of v1, /device:TPU:0, one launch (start us, length us, event | category | flops | bytes accessed | tf_op | source)
XLA Modules:
  0.0 210.2 jit_solution(7210298670685279767)
XLA Ops:
  1.4 4.9 %collective-permute-start = (f32[2,25,128]{2,1,0:T(8,128)S(1)}, f32[2,25,128]{2,1,0:T(8,128)S(1)}, u32[]{:S(2)}, u32[]{:S(2)}) collective-permute-start(f32[2,25,128]{2,1,0:T(8,128)S(1)} %get-tuple-element.62), channel_id=1, source_target_pairs={{0,4},{1,5},{2,6},{3,7},{8,12},{9,13},{10,14},{11,15},{16,20},{17,... | collective-permute-start | bytes 76808 | tf_op jit(solution)/shard_map/ppermute | solution.py:31
  8.8 3.6 %collective-permute-start.4 = (f32[1,512,128]{2,1,0:T(8,128)S(1)}, f32[1,512,128]{2,1,0:T(8,128)S(1)}, u32[]{:S(2)}, u32[]{:S(2)}) collective-permute-start(f32[1,512,128]{2,1,0:T(8,128)S(1)} %get-tuple-element.58), channel_id=1, source_target_pairs={{0,8},{8,16},{16,24},{1,9},{9,17},{17,25},{2,10},{10,18},{18,26},{... | collective-permute-start | bytes 786440 | tf_op jit(solution)/shard_map/ppermute | solution.py:43
  16.2 3.7 %collective-permute-done.3 = f32[2,512,25]{1,2,0:T(8,128)S(1)} collective-permute-done((f32[2,512,25]{1,2,0:T(8,128)S(1)}, f32[2,512,25]{1,2,0:T(8,128)S(1)}, u32[]{:S(2)}, u32[]{:S(2)}) %collective-permute-start.3) | collective-permute-done | bytes 102432 | tf_op jit(solution)/shard_map/ppermute | solution.py:33
  20.0 2.5 %multiply_reduce_fusion.6 = (f32[]{:T(128)}, f32[2,512,128]{2,1,0:T(8,128)S(1)}, f32[2,512,128]{2,1,0:T(8,128)}) fusion(f32[2,512,128]{2,1,0:T(8,128)S(1)} %copy-done.8, f32[2,512,128]{2,1,0:T(8,128)S(1)} %copy-done.1, f32[2,512,128]{2,1,0:T(8,128)S(1)} %broadcast_multiply_fusion, f32[1,512,128]{2,1,0:T(8,128)S(1)} %get-tuple-element.59, ...), kind=kOutput, calls=%fused_computation.144 | convolution fusion | flops 282915840 | bytes 5447684 | tf_op jit(solution)/shard_map/liq,qj->lij/dot_general | solution.py:58
  22.5 4.5 %collective-permute-start.5 = (f32[2,25,128]{2,1,0:T(8,128)S(1)}, f32[2,25,128]{2,1,0:T(8,128)S(1)}, u32[]{:S(2)}, u32[]{:S(2)}) collective-permute-start(f32[2,25,128]{2,1,0:T(8,128)S(1)} %get-tuple-element.56), channel_id=1, source_target_pairs={{0,4},{1,5},{2,6},{3,7},{8,12},{9,13},{10,14},{11,15},{16,20},{17,... | collective-permute-start | bytes 76808 | tf_op jit(solution)/shard_map/ppermute | solution.py:31
  28.6 4.2 %collective-permute-done.6 = f32[2,25,128]{2,1,0:T(8,128)S(1)} collective-permute-done((f32[2,25,128]{2,1,0:T(8,128)S(1)}, f32[2,25,128]{2,1,0:T(8,128)S(1)}, u32[]{:S(2)}, u32[]{:S(2)}) %collective-permute-start.6) | collective-permute-done | bytes 25632 | tf_op jit(solution)/shard_map/ppermute | solution.py:33
  33.8 4.0 %collective-permute-start.7 = (f32[2,512,25]{1,2,0:T(8,128)S(1)}, f32[2,512,25]{1,2,0:T(8,128)S(1)}, u32[]{:S(2)}, u32[]{:S(2)}) collective-permute-start(f32[2,512,25]{1,2,0:T(8,128)S(1)} %get-tuple-element.54), channel_id=1, source_target_pairs={{0,1},{1,2},{2,3},{4,5},{5,6},{6,7},{8,9},{9,10},{10,11},{12,13},{... | collective-permute-start | bytes 307208 | tf_op jit(solution)/shard_map/ppermute | solution.py:31
  41.9 1.7 multiply_reduce_fusion.8
  43.6 1.6 collective-permute-start.10
  46.8 4.2 %collective-permute-done.11 = f32[2,25,128]{2,1,0:T(8,128)S(1)} collective-permute-done((f32[2,25,128]{2,1,0:T(8,128)S(1)}, f32[2,25,128]{2,1,0:T(8,128)S(1)}, u32[]{:S(2)}, u32[]{:S(2)}) %collective-permute-start.11) | collective-permute-done | bytes 25632 | tf_op jit(solution)/shard_map/ppermute | solution.py:33
  52.9 3.5 %collective-permute-start.14 = (f32[1,512,128]{2,1,0:T(8,128)S(1)}, f32[1,512,128]{2,1,0:T(8,128)S(1)}, u32[]{:S(2)}, u32[]{:S(2)}) collective-permute-start(f32[1,512,128]{2,1,0:T(8,128)S(1)} %get-tuple-element.46), channel_id=1, source_target_pairs={{0,8},{8,16},{16,24},{1,9},{9,17},{17,25},{2,10},{10,18},{18,26},{... | collective-permute-start | bytes 786440 | tf_op jit(solution)/shard_map/ppermute | solution.py:43
  57.1 4.7 %collective-permute-start.12 = (f32[2,512,25]{1,2,0:T(8,128)}, f32[2,512,25]{1,2,0:T(8,128)}, u32[]{:S(2)}, u32[]{:S(2)}) collective-permute-start(f32[2,512,25]{1,2,0:T(8,128)} %get-tuple-element.50), channel_id=1, source_target_pairs={{0,1},{1,2},{2,3},{4,5},{5,6},{6,7},{8,9},{9,10},{10,11},{12,13},{... | collective-permute-start | bytes 307208 | tf_op jit(solution)/shard_map/ppermute | solution.py:31
  64.3 10.6 %all-reduce.5 = (f32[]{:T(128)}, f32[]{:T(128)}) all-reduce(f32[]{:T(128)S(6)} %add.127, f32[]{:T(128)} %get-tuple-element.26), channel_id=1, replica_groups=mesh['layer'=4,'row'=2,'col'=4] {'layer'}, use_global_device_ids=true, to_apply=%region_2.3 | all-reduce | flops 2 | bytes 16 | tf_op jit(solution)/shard_map/psum | solution.py:19
  75.0 12.4 %all-reduce.2 = (f32[]{:T(128)}, f32[]{:T(128)}) all-reduce(f32[]{:T(128)} %get-tuple-element.14, f32[]{:T(128)} %get-tuple-element.15), channel_id=1, replica_groups=mesh['layer'=4,'row'=2,'col'=4] {'row','col'}, use_global_device_ids=true, to_apply=%region_3.4 | all-reduce | flops 2 | bytes 16 | tf_op jit(solution)/shard_map/psum | solution.py:19
  89.5 3.9 %multiply_reduce_fusion.3 = (f32[]{:T(128)}, f32[2,512,128]{2,1,0:T(8,128)S(1)}, f32[2,512,128]{2,1,0:T(8,128)}) fusion(f32[2,512,128]{2,1,0:T(8,128)} %get-tuple-element.64, f32[2,512,128]{2,1,0:T(8,128)S(1)} %copy-done.1, f32[2,512,128]{2,1,0:T(8,128)S(1)} %get-tuple-element.21, f32[1,512,128]{2,1,0:T(8,128)S(1)} %get-tuple-element.47, ...), kind=kOutput, calls=%fused_computation.139 | convolution fusion | flops 282915840 | bytes 5447688 | tf_op jit(solution)/shard_map/liq,qj->lij/dot_general | solution.py:58
  93.4 3.2 %collective-permute-start.15 = (f32[2,25,128]{2,1,0:T(8,128)S(1)}, f32[2,25,128]{2,1,0:T(8,128)S(1)}, u32[]{:S(2)}, u32[]{:S(2)}) collective-permute-start(f32[2,25,128]{2,1,0:T(8,128)S(1)} %get-tuple-element.44), channel_id=1, source_target_pairs={{0,4},{1,5},{2,6},{3,7},{8,12},{9,13},{10,14},{11,15},{16,20},{17,... | collective-permute-start | bytes 76808 | tf_op jit(solution)/shard_map/ppermute | solution.py:31
  98.2 4.2 %collective-permute-done.16 = f32[2,25,128]{2,1,0:T(8,128)S(1)} collective-permute-done((f32[2,25,128]{2,1,0:T(8,128)S(1)}, f32[2,25,128]{2,1,0:T(8,128)S(1)}, u32[]{:S(2)}, u32[]{:S(2)}) %collective-permute-start.16) | collective-permute-done | bytes 25632 | tf_op jit(solution)/shard_map/ppermute | solution.py:33
  108.1 1.7 multiply_reduce_fusion.5
  109.8 1.6 collective-permute-start.20
  113.0 4.2 %collective-permute-done.21 = f32[2,25,128]{2,1,0:T(8,128)S(1)} collective-permute-done((f32[2,25,128]{2,1,0:T(8,128)S(1)}, f32[2,25,128]{2,1,0:T(8,128)S(1)}, u32[]{:S(2)}, u32[]{:S(2)}) %collective-permute-start.21) | collective-permute-done | bytes 25632 | tf_op jit(solution)/shard_map/ppermute | solution.py:33
  119.1 4.1 %collective-permute-start.24 = (f32[1,512,128]{2,1,0:T(8,128)S(1)}, f32[1,512,128]{2,1,0:T(8,128)S(1)}, u32[]{:S(2)}, u32[]{:S(2)}) collective-permute-start(f32[1,512,128]{2,1,0:T(8,128)S(1)} %get-tuple-element.34), channel_id=1, source_target_pairs={{0,8},{8,16},{16,24},{1,9},{9,17},{17,25},{2,10},{10,18},{18,26},{... | collective-permute-start | bytes 786440 | tf_op jit(solution)/shard_map/ppermute | solution.py:43
  124.0 2.6 %collective-permute-start.22 = (f32[2,512,25]{1,2,0:T(8,128)}, f32[2,512,25]{1,2,0:T(8,128)}, u32[]{:S(2)}, u32[]{:S(2)}) collective-permute-start(f32[2,512,25]{1,2,0:T(8,128)} %get-tuple-element.38), channel_id=1, source_target_pairs={{0,1},{1,2},{2,3},{4,5},{5,6},{6,7},{8,9},{9,10},{10,11},{12,13},{... | collective-permute-start | bytes 307208 | tf_op jit(solution)/shard_map/ppermute | solution.py:31
  129.1 9.3 %all-reduce.4 = (f32[]{:T(128)}, f32[]{:T(128)}) all-reduce(f32[]{:T(128)S(6)} %add.136, f32[]{:T(128)} %get-tuple-element.24), channel_id=1, replica_groups=mesh['layer'=4,'row'=2,'col'=4] {'layer'}, use_global_device_ids=true, to_apply=%region_9.10 | all-reduce | flops 2 | bytes 16 | tf_op jit(solution)/shard_map/psum | solution.py:19
  138.4 14.0 %all-reduce.1 = (f32[]{:T(128)}, f32[]{:T(128)}) all-reduce(f32[]{:T(128)} %get-tuple-element.12, f32[]{:T(128)} %get-tuple-element.13), channel_id=1, replica_groups=mesh['layer'=4,'row'=2,'col'=4] {'row','col'}, use_global_device_ids=true, to_apply=%region_10.11 | all-reduce | flops 2 | bytes 16 | tf_op jit(solution)/shard_map/psum | solution.py:19
  154.5 3.9 %multiply_reduce_fusion = (f32[]{:T(128)}, f32[2,512,128]{2,1,0:T(8,128)S(1)}, f32[2,512,128]{2,1,0:T(8,128)}) fusion(f32[2,512,128]{2,1,0:T(8,128)} %get-tuple-element.67, f32[2,512,128]{2,1,0:T(8,128)S(1)} %copy-done.1, f32[2,512,128]{2,1,0:T(8,128)S(1)} %get-tuple-element.19, f32[1,512,128]{2,1,0:T(8,128)S(1)} %get-tuple-element.35, ...), kind=kOutput, calls=%fused_computation.134 | convolution fusion | flops 282915840 | bytes 5447688 | tf_op jit(solution)/shard_map/liq,qj->lij/dot_general | solution.py:58
  158.4 3.2 %collective-permute-start.25 = (f32[2,25,128]{2,1,0:T(8,128)S(1)}, f32[2,25,128]{2,1,0:T(8,128)S(1)}, u32[]{:S(2)}, u32[]{:S(2)}) collective-permute-start(f32[2,25,128]{2,1,0:T(8,128)S(1)} %get-tuple-element.32), channel_id=1, source_target_pairs={{0,4},{1,5},{2,6},{3,7},{8,12},{9,13},{10,14},{11,15},{16,20},{17,... | collective-permute-start | bytes 76808 | tf_op jit(solution)/shard_map/ppermute | solution.py:31
  163.2 4.2 %collective-permute-done.26 = f32[2,25,128]{2,1,0:T(8,128)S(1)} collective-permute-done((f32[2,25,128]{2,1,0:T(8,128)S(1)}, f32[2,25,128]{2,1,0:T(8,128)S(1)}, u32[]{:S(2)}, u32[]{:S(2)}) %collective-permute-start.26) | collective-permute-done | bytes 25632 | tf_op jit(solution)/shard_map/ppermute | solution.py:33
  173.1 2.5 %multiply_reduce_fusion.2 = (f32[]{:T(128)}, f32[2,512,128]{2,1,0:T(8,128)}) fusion(f32[2,512,128]{2,1,0:T(8,128)S(1)} %copy-done.13, pred[2,512,128]{2,1,0:T(32,128)(4,1)S(1)} %broadcast_compare_fusion, f32[2,512,25]{1,2,0:T(8,128)S(1)} %collective-permute-done.28, f32[2,512,128]{1,2,0:T(8,128)S(1)} %convolution_bitcast_fusion, ...), kind=kOutput, calls=%fused_computation.136 | convolution fusion | flops 281867264 | bytes 1908744 | tf_op jit(solution)/shard_map/liq,qj->lij/dot_general | solution.py:58
  175.6 6.5 %collective-permute-done.29 = f32[1,512,128]{2,1,0:T(8,128)S(1)} collective-permute-done((f32[1,512,128]{2,1,0:T(8,128)S(1)}, f32[1,512,128]{2,1,0:T(8,128)S(1)}, u32[]{:S(2)}, u32[]{:S(2)}) %collective-permute-start.29) | collective-permute-done | bytes 262176 | tf_op jit(solution)/shard_map/ppermute | solution.py:43
  182.1 1.6 multiply_reduce_fusion.1
  184.9 10.4 %all-reduce.3 = (f32[]{:T(128)}, f32[]{:T(128)}) all-reduce(f32[]{:T(128)S(6)} %add.145, f32[]{:T(128)} %get-tuple-element.22), channel_id=1, replica_groups=mesh['layer'=4,'row'=2,'col'=4] {'layer'}, use_global_device_ids=true, to_apply=%region_16.17 | all-reduce | flops 2 | bytes 16 | tf_op jit(solution)/shard_map/psum | solution.py:19
  195.4 12.4 %all-reduce = (f32[]{:T(128)}, f32[]{:T(128)}) all-reduce(f32[]{:T(128)} %get-tuple-element.10, f32[]{:T(128)} %get-tuple-element.11), channel_id=1, replica_groups=mesh['layer'=4,'row'=2,'col'=4] {'row','col'}, use_global_device_ids=true, to_apply=%region_17.18 | all-reduce | flops 2 | bytes 16 | tf_op jit(solution)/shard_map/psum | solution.py:19
  (103 shorter events, 40.0 us)
Async XLA Ops:
  1.4 11.0 %collective-permute-start = (f32[2,25,128]{2,1,0:T(8,128)S(1)}, f32[2,25,128]{2,1,0:T(8,128)S(1)}, u32[]{:S(2)}, u32[]{:S(2)}) collective-permute-start(f32[2,25,128]{2,1,0:T(8,128)S(1)} %get-tuple-element.62), channel_id=1, source_target_pairs={{0,4},{1,5},{2,6},{3,7},{8,12},{9,13},{10,14},{11,15},{16,20},{17,... | collective-permute-start | bytes 76808 | tf_op jit(solution)/shard_map/ppermute | solution.py:31
  6.3 6.2 %collective-permute-start.1 = (f32[2,25,128]{2,1,0:T(8,128)S(1)}, f32[2,25,128]{2,1,0:T(8,128)S(1)}, u32[]{:S(2)}, u32[]{:S(2)}) collective-permute-start(f32[2,25,128]{2,1,0:T(8,128)S(1)} %get-tuple-element.63), channel_id=1, source_target_pairs={{4,0},{5,1},{6,2},{7,3},{12,8},{13,9},{14,10},{15,11},{20,16},{21,... | collective-permute-start | bytes 76808 | tf_op jit(solution)/shard_map/ppermute | solution.py:33
  8.8 11.1 %collective-permute-start.4 = (f32[1,512,128]{2,1,0:T(8,128)S(1)}, f32[1,512,128]{2,1,0:T(8,128)S(1)}, u32[]{:S(2)}, u32[]{:S(2)}) collective-permute-start(f32[1,512,128]{2,1,0:T(8,128)S(1)} %get-tuple-element.58), channel_id=1, source_target_pairs={{0,8},{8,16},{16,24},{1,9},{9,17},{17,25},{2,10},{10,18},{18,26},{... | collective-permute-start | bytes 786440 | tf_op jit(solution)/shard_map/ppermute | solution.py:43
  13.5 2.7 %collective-permute-start.2 = (f32[2,512,25]{1,2,0:T(8,128)S(1)}, f32[2,512,25]{1,2,0:T(8,128)S(1)}, u32[]{:S(2)}, u32[]{:S(2)}) collective-permute-start(f32[2,512,25]{1,2,0:T(8,128)S(1)} %get-tuple-element.60), channel_id=1, source_target_pairs={{0,1},{1,2},{2,3},{4,5},{5,6},{6,7},{8,9},{9,10},{10,11},{12,13},{... | collective-permute-start | bytes 307208 | tf_op jit(solution)/shard_map/ppermute | solution.py:31
  14.9 5.0 %collective-permute-start.3 = (f32[2,512,25]{1,2,0:T(8,128)S(1)}, f32[2,512,25]{1,2,0:T(8,128)S(1)}, u32[]{:S(2)}, u32[]{:S(2)}) collective-permute-start(f32[2,512,25]{1,2,0:T(8,128)S(1)} %get-tuple-element.61), channel_id=1, source_target_pairs={{1,0},{2,1},{3,2},{5,4},{6,5},{7,6},{9,8},{10,9},{11,10},{13,12},{... | collective-permute-start | bytes 307208 | tf_op jit(solution)/shard_map/ppermute | solution.py:33
  22.5 6.1 %collective-permute-start.5 = (f32[2,25,128]{2,1,0:T(8,128)S(1)}, f32[2,25,128]{2,1,0:T(8,128)S(1)}, u32[]{:S(2)}, u32[]{:S(2)}) collective-permute-start(f32[2,25,128]{2,1,0:T(8,128)S(1)} %get-tuple-element.56), channel_id=1, source_target_pairs={{0,4},{1,5},{2,6},{3,7},{8,12},{9,13},{10,14},{11,15},{16,20},{17,... | collective-permute-start | bytes 76808 | tf_op jit(solution)/shard_map/ppermute | solution.py:31
  27.0 5.8 %collective-permute-start.6 = (f32[2,25,128]{2,1,0:T(8,128)S(1)}, f32[2,25,128]{2,1,0:T(8,128)S(1)}, u32[]{:S(2)}, u32[]{:S(2)}) collective-permute-start(f32[2,25,128]{2,1,0:T(8,128)S(1)} %get-tuple-element.57), channel_id=1, source_target_pairs={{4,0},{5,1},{6,2},{7,3},{12,8},{13,9},{14,10},{15,11},{20,16},{21,... | collective-permute-start | bytes 76808 | tf_op jit(solution)/shard_map/ppermute | solution.py:33
  33.8 6.7 %collective-permute-start.7 = (f32[2,512,25]{1,2,0:T(8,128)S(1)}, f32[2,512,25]{1,2,0:T(8,128)S(1)}, u32[]{:S(2)}, u32[]{:S(2)}) collective-permute-start(f32[2,512,25]{1,2,0:T(8,128)S(1)} %get-tuple-element.54), channel_id=1, source_target_pairs={{0,1},{1,2},{2,3},{4,5},{5,6},{6,7},{8,9},{9,10},{10,11},{12,13},{... | collective-permute-start | bytes 307208 | tf_op jit(solution)/shard_map/ppermute | solution.py:31
  37.8 4.0 %collective-permute-start.8 = (f32[2,512,25]{1,2,0:T(8,128)S(1)}, f32[2,512,25]{1,2,0:T(8,128)S(1)}, u32[]{:S(2)}, u32[]{:S(2)}) collective-permute-start(f32[2,512,25]{1,2,0:T(8,128)S(1)} %get-tuple-element.55), channel_id=1, source_target_pairs={{1,0},{2,1},{3,2},{5,4},{6,5},{7,6},{9,8},{10,9},{11,10},{13,12},{... | collective-permute-start | bytes 307208 | tf_op jit(solution)/shard_map/ppermute | solution.py:33
  39.2 12.8 %collective-permute-start.9 = (f32[1,512,128]{2,1,0:T(8,128)S(1)}, f32[1,512,128]{2,1,0:T(8,128)S(1)}, u32[]{:S(2)}, u32[]{:S(2)}) collective-permute-start(f32[1,512,128]{2,1,0:T(8,128)S(1)} %get-tuple-element.49), channel_id=1, source_target_pairs={{8,0},{16,8},{24,16},{9,1},{17,9},{25,17},{10,2},{18,10},{26,18},{... | collective-permute-start | bytes 786440 | tf_op jit(solution)/shard_map/ppermute | solution.py:43
  43.5 8.4 %copy-start.14 = (f32[2,512,128]{2,1,0:T(8,128)}, f32[2,512,128]{2,1,0:T(8,128)S(1)}, u32[]{:S(2)}) copy-start(f32[2,512,128]{2,1,0:T(8,128)S(1)} %get-tuple-element.66) | copy-start | bytes 1572868
  43.6 3.2 %collective-permute-start.10 = (f32[2,25,128]{2,1,0:T(8,128)S(1)}, f32[2,25,128]{2,1,0:T(8,128)S(1)}, u32[]{:S(2)}, u32[]{:S(2)}) collective-permute-start(f32[2,25,128]{2,1,0:T(8,128)S(1)} %get-tuple-element.52), channel_id=1, source_target_pairs={{0,4},{1,5},{2,6},{3,7},{8,12},{9,13},{10,14},{11,15},{16,20},{17,... | collective-permute-start | bytes 76808 | tf_op jit(solution)/shard_map/ppermute | solution.py:31
  45.2 5.8 %collective-permute-start.11 = (f32[2,25,128]{2,1,0:T(8,128)S(1)}, f32[2,25,128]{2,1,0:T(8,128)S(1)}, u32[]{:S(2)}, u32[]{:S(2)}) collective-permute-start(f32[2,25,128]{2,1,0:T(8,128)S(1)} %get-tuple-element.53), channel_id=1, source_target_pairs={{4,0},{5,1},{6,2},{7,3},{12,8},{13,9},{14,10},{15,11},{20,16},{21,... | collective-permute-start | bytes 76808 | tf_op jit(solution)/shard_map/ppermute | solution.py:33
  52.9 35.9 %collective-permute-start.14 = (f32[1,512,128]{2,1,0:T(8,128)S(1)}, f32[1,512,128]{2,1,0:T(8,128)S(1)}, u32[]{:S(2)}, u32[]{:S(2)}) collective-permute-start(f32[1,512,128]{2,1,0:T(8,128)S(1)} %get-tuple-element.46), channel_id=1, source_target_pairs={{0,8},{8,16},{16,24},{1,9},{9,17},{17,25},{2,10},{10,18},{18,26},{... | collective-permute-start | bytes 786440 | tf_op jit(solution)/shard_map/ppermute | solution.py:43
  57.1 31.6 %collective-permute-start.12 = (f32[2,512,25]{1,2,0:T(8,128)}, f32[2,512,25]{1,2,0:T(8,128)}, u32[]{:S(2)}, u32[]{:S(2)}) collective-permute-start(f32[2,512,25]{1,2,0:T(8,128)} %get-tuple-element.50), channel_id=1, source_target_pairs={{0,1},{1,2},{2,3},{4,5},{5,6},{6,7},{8,9},{9,10},{10,11},{12,13},{... | collective-permute-start | bytes 307208 | tf_op jit(solution)/shard_map/ppermute | solution.py:31
  61.8 26.9 %collective-permute-start.13 = (f32[2,512,25]{1,2,0:T(8,128)}, f32[2,512,25]{1,2,0:T(8,128)}, u32[]{:S(2)}, u32[]{:S(2)}) collective-permute-start(f32[2,512,25]{1,2,0:T(8,128)} %get-tuple-element.51), channel_id=1, source_target_pairs={{1,0},{2,1},{3,2},{5,4},{6,5},{7,6},{9,8},{10,9},{11,10},{13,12},{... | collective-permute-start | bytes 307208 | tf_op jit(solution)/shard_map/ppermute | solution.py:33
  93.4 4.8 %collective-permute-start.15 = (f32[2,25,128]{2,1,0:T(8,128)S(1)}, f32[2,25,128]{2,1,0:T(8,128)S(1)}, u32[]{:S(2)}, u32[]{:S(2)}) collective-permute-start(f32[2,25,128]{2,1,0:T(8,128)S(1)} %get-tuple-element.44), channel_id=1, source_target_pairs={{0,4},{1,5},{2,6},{3,7},{8,12},{9,13},{10,14},{11,15},{16,20},{17,... | collective-permute-start | bytes 76808 | tf_op jit(solution)/shard_map/ppermute | solution.py:31
  96.6 5.8 %collective-permute-start.16 = (f32[2,25,128]{2,1,0:T(8,128)S(1)}, f32[2,25,128]{2,1,0:T(8,128)S(1)}, u32[]{:S(2)}, u32[]{:S(2)}) collective-permute-start(f32[2,25,128]{2,1,0:T(8,128)S(1)} %get-tuple-element.45), channel_id=1, source_target_pairs={{4,0},{5,1},{6,2},{7,3},{12,8},{13,9},{14,10},{15,11},{20,16},{21,... | collective-permute-start | bytes 76808 | tf_op jit(solution)/shard_map/ppermute | solution.py:33
  103.4 4.1 %collective-permute-start.17 = (f32[2,512,25]{1,2,0:T(8,128)S(1)}, f32[2,512,25]{1,2,0:T(8,128)S(1)}, u32[]{:S(2)}, u32[]{:S(2)}) collective-permute-start(f32[2,512,25]{1,2,0:T(8,128)S(1)} %get-tuple-element.42), channel_id=1, source_target_pairs={{0,1},{1,2},{2,3},{4,5},{5,6},{6,7},{8,9},{9,10},{10,11},{12,13},{... | collective-permute-start | bytes 307208 | tf_op jit(solution)/shard_map/ppermute | solution.py:31
  104.7 3.4 %collective-permute-start.18 = (f32[2,512,25]{1,2,0:T(8,128)S(1)}, f32[2,512,25]{1,2,0:T(8,128)S(1)}, u32[]{:S(2)}, u32[]{:S(2)}) collective-permute-start(f32[2,512,25]{1,2,0:T(8,128)S(1)} %get-tuple-element.43), channel_id=1, source_target_pairs={{1,0},{2,1},{3,2},{5,4},{6,5},{7,6},{9,8},{10,9},{11,10},{13,12},{... | collective-permute-start | bytes 307208 | tf_op jit(solution)/shard_map/ppermute | solution.py:33
  106.2 12.0 %collective-permute-start.19 = (f32[1,512,128]{2,1,0:T(8,128)S(1)}, f32[1,512,128]{2,1,0:T(8,128)S(1)}, u32[]{:S(2)}, u32[]{:S(2)}) collective-permute-start(f32[1,512,128]{2,1,0:T(8,128)S(1)} %get-tuple-element.37), channel_id=1, source_target_pairs={{8,0},{16,8},{24,16},{9,1},{17,9},{25,17},{10,2},{18,10},{26,18},{... | collective-permute-start | bytes 786440 | tf_op jit(solution)/shard_map/ppermute | solution.py:43
  109.8 3.2 %collective-permute-start.20 = (f32[2,25,128]{2,1,0:T(8,128)S(1)}, f32[2,25,128]{2,1,0:T(8,128)S(1)}, u32[]{:S(2)}, u32[]{:S(2)}) collective-permute-start(f32[2,25,128]{2,1,0:T(8,128)S(1)} %get-tuple-element.40), channel_id=1, source_target_pairs={{0,4},{1,5},{2,6},{3,7},{8,12},{9,13},{10,14},{11,15},{16,20},{17,... | collective-permute-start | bytes 76808 | tf_op jit(solution)/shard_map/ppermute | solution.py:31
  111.4 5.8 %collective-permute-start.21 = (f32[2,25,128]{2,1,0:T(8,128)S(1)}, f32[2,25,128]{2,1,0:T(8,128)S(1)}, u32[]{:S(2)}, u32[]{:S(2)}) collective-permute-start(f32[2,25,128]{2,1,0:T(8,128)S(1)} %get-tuple-element.41), channel_id=1, source_target_pairs={{4,0},{5,1},{6,2},{7,3},{12,8},{13,9},{14,10},{15,11},{20,16},{21,... | collective-permute-start | bytes 76808 | tf_op jit(solution)/shard_map/ppermute | solution.py:33
  119.1 35.4 %copy-start.4 = (s32[2,512,128]{2,1,0:T(8,128)S(1)}, s32[2,512,128]{2,1,0:T(8,128)}, u32[]{:S(2)}) copy-start(s32[2,512,128]{2,1,0:T(8,128)} %param.9) | copy-start | bytes 1572868
  119.1 34.7 %collective-permute-start.24 = (f32[1,512,128]{2,1,0:T(8,128)S(1)}, f32[1,512,128]{2,1,0:T(8,128)S(1)}, u32[]{:S(2)}, u32[]{:S(2)}) collective-permute-start(f32[1,512,128]{2,1,0:T(8,128)S(1)} %get-tuple-element.34), channel_id=1, source_target_pairs={{0,8},{8,16},{16,24},{1,9},{9,17},{17,25},{2,10},{10,18},{18,26},{... | collective-permute-start | bytes 786440 | tf_op jit(solution)/shard_map/ppermute | solution.py:43
  124.0 29.8 %collective-permute-start.22 = (f32[2,512,25]{1,2,0:T(8,128)}, f32[2,512,25]{1,2,0:T(8,128)}, u32[]{:S(2)}, u32[]{:S(2)}) collective-permute-start(f32[2,512,25]{1,2,0:T(8,128)} %get-tuple-element.38), channel_id=1, source_target_pairs={{0,1},{1,2},{2,3},{4,5},{5,6},{6,7},{8,9},{9,10},{10,11},{12,13},{... | collective-permute-start | bytes 307208 | tf_op jit(solution)/shard_map/ppermute | solution.py:31
  126.6 27.2 %collective-permute-start.23 = (f32[2,512,25]{1,2,0:T(8,128)}, f32[2,512,25]{1,2,0:T(8,128)}, u32[]{:S(2)}, u32[]{:S(2)}) collective-permute-start(f32[2,512,25]{1,2,0:T(8,128)} %get-tuple-element.39), channel_id=1, source_target_pairs={{1,0},{2,1},{3,2},{5,4},{6,5},{7,6},{9,8},{10,9},{11,10},{13,12},{... | collective-permute-start | bytes 307208 | tf_op jit(solution)/shard_map/ppermute | solution.py:33
  158.4 4.8 %collective-permute-start.25 = (f32[2,25,128]{2,1,0:T(8,128)S(1)}, f32[2,25,128]{2,1,0:T(8,128)S(1)}, u32[]{:S(2)}, u32[]{:S(2)}) collective-permute-start(f32[2,25,128]{2,1,0:T(8,128)S(1)} %get-tuple-element.32), channel_id=1, source_target_pairs={{0,4},{1,5},{2,6},{3,7},{8,12},{9,13},{10,14},{11,15},{16,20},{17,... | collective-permute-start | bytes 76808 | tf_op jit(solution)/shard_map/ppermute | solution.py:31
  161.7 5.8 %collective-permute-start.26 = (f32[2,25,128]{2,1,0:T(8,128)S(1)}, f32[2,25,128]{2,1,0:T(8,128)S(1)}, u32[]{:S(2)}, u32[]{:S(2)}) collective-permute-start(f32[2,25,128]{2,1,0:T(8,128)S(1)} %get-tuple-element.33), channel_id=1, source_target_pairs={{4,0},{5,1},{6,2},{7,3},{12,8},{13,9},{14,10},{15,11},{20,16},{21,... | collective-permute-start | bytes 76808 | tf_op jit(solution)/shard_map/ppermute | solution.py:33
  168.4 4.1 %collective-permute-start.27 = (f32[2,512,25]{1,2,0:T(8,128)S(1)}, f32[2,512,25]{1,2,0:T(8,128)S(1)}, u32[]{:S(2)}, u32[]{:S(2)}) collective-permute-start(f32[2,512,25]{1,2,0:T(8,128)S(1)} %get-tuple-element.30), channel_id=1, source_target_pairs={{0,1},{1,2},{2,3},{4,5},{5,6},{6,7},{8,9},{9,10},{10,11},{12,13},{... | collective-permute-start | bytes 307208 | tf_op jit(solution)/shard_map/ppermute | solution.py:31
  169.7 3.4 %collective-permute-start.28 = (f32[2,512,25]{1,2,0:T(8,128)S(1)}, f32[2,512,25]{1,2,0:T(8,128)S(1)}, u32[]{:S(2)}, u32[]{:S(2)}) collective-permute-start(f32[2,512,25]{1,2,0:T(8,128)S(1)} %get-tuple-element.31), channel_id=1, source_target_pairs={{1,0},{2,1},{3,2},{5,4},{6,5},{7,6},{9,8},{10,9},{11,10},{13,12},{... | collective-permute-start | bytes 307208 | tf_op jit(solution)/shard_map/ppermute | solution.py:33
  171.2 10.9 %collective-permute-start.29 = (f32[1,512,128]{2,1,0:T(8,128)S(1)}, f32[1,512,128]{2,1,0:T(8,128)S(1)}, u32[]{:S(2)}, u32[]{:S(2)}) collective-permute-start(f32[1,512,128]{2,1,0:T(8,128)S(1)} %get-tuple-element.29), channel_id=1, source_target_pairs={{8,0},{16,8},{24,16},{9,1},{17,9},{25,17},{10,2},{18,10},{26,18},{... | collective-permute-start | bytes 786440 | tf_op jit(solution)/shard_map/ppermute | solution.py:43
  (14 other events, 71.5 us)
